TPU v7x, 32 devices: a whole 2x2x4 slice. The times are simulated.
32 devices in a mesh: row: 4 (over z), col: 8 (over y, x, core).
Axes of the slice: x: 2, y: 2, z: 4, core: 2. Of those that a mesh axis runs over, the one named last changes fastest.
Arguments:
- object_amplitude: float32 [1024, 2048], P('row', 'col'), may hold values from 0.3 to 3
- object_phase: float32 [1024, 2048], P('row', 'col'), may hold values from -3.140625 to 3.140625
- probe: float32 [4, 2, 256, 256], replicated, may hold values from -6 to 6
- amplitudes: float32 [256, 256, 256], P(('row', 'col')), may hold values from 0.5 to 3
- positions: int32 [256, 2], P(('row', 'col')), may hold values from -64 to 64
Outputs:
- new_object: float32 [2, 1024, 2048], P(None, 'row', 'col')
- new_probe: float32 [4, 2, 256, 256], replicated
Inputs may be any that keep to these rules, and one draw needn't show every extreme that they name: `positions`: row and column offsets of each frame's first pixel from the first pixel of its owner tile f // 8, tiles row-major; both ends of the range occur.
All inputs are finite; a program needn't handle non-finite values.
Results may differ from a plain program's by a relative error of at most 0.0014.
The roundings to bfloat16 on the way count: a program that leaves them out, or rounds other values in their place, can miss the bound.
Values sent between devices are 32-bit elements; how exact they have to be, the bound alone decides.
A program may use at most 192 MiB of HBM per device.

v0:
```python
import math
import jax
import jax.numpy as jnp
from jax import lax
from jax.sharding import PartitionSpec as P

H = 64


def extended_2(block, sides, width):
    for axis, dim in sides:
        count = lax.axis_size(axis)
        forward = [(i, i + 1) for i in range(count - 1)]
        backward = [(target, source) for source, target in forward]
        low = lax.ppermute(
            lax.slice_in_dim(block, block.shape[dim] - width, None, axis=dim), axis, forward
        )
        high = lax.ppermute(lax.slice_in_dim(block, 0, width, axis=dim), axis, backward)
        block = jnp.concatenate([low, block, high], axis=dim)
    return block


def fourier_table(frame_side, exponent_sign):
    counter = jnp.arange(frame_side, dtype=jnp.int32)
    product = counter[:, None] * counter[None, :] % frame_side
    phase_angle = product.astype(jnp.float32) * (2.0 * math.pi / frame_side)
    norming = 1.0 / math.sqrt(frame_side)
    real_part = jnp.cos(phase_angle) * norming
    imaginary = exponent_sign * jnp.sin(phase_angle) * norming
    upper_rows = jnp.stack([real_part, -imaginary], axis=1)
    lower_rows = jnp.stack([imaginary, real_part], axis=1)
    return jnp.stack([upper_rows, lower_rows], axis=0).astype(jnp.bfloat16)


def transform(matrix, values):
    halfway = jnp.einsum("akcy,fmcyx->fmakx", matrix, values, preferred_element_type=jnp.float32)
    return jnp.einsum(
        "fmakx,blax->fmbkl",
        halfway.astype(jnp.bfloat16),
        matrix,
        preferred_element_type=jnp.float32,
    )


def frame_terms(patches, probe, measured, forward, inverse):
    object_real = patches[:, None, 0]
    object_imag = patches[:, None, 1]
    probe_real = probe[None, :, 0]
    probe_imag = probe[None, :, 1]
    exit_wave = jnp.stack(
        [
            probe_real * object_real - probe_imag * object_imag,
            probe_real * object_imag + probe_imag * object_real,
        ],
        axis=2,
    )
    spectrum = transform(forward, exit_wave.astype(jnp.bfloat16))
    intensity = jnp.sum(spectrum * spectrum, axis=(1, 2))
    factor = measured / jnp.maximum(jnp.sqrt(intensity), 1.0)
    corrected = (spectrum * factor[:, None, None]).astype(jnp.bfloat16)
    returned = transform(inverse, corrected)
    change = returned - exit_wave
    change_real = change[:, :, 0]
    change_imag = change[:, :, 1]
    object_gradient = jnp.stack(
        [
            jnp.sum(probe_real * change_real + probe_imag * change_imag, axis=1),
            jnp.sum(probe_real * change_imag - probe_imag * change_real, axis=1),
        ],
        axis=1,
    )
    probe_gradient = jnp.stack(
        [
            jnp.sum(object_real * change_real + object_imag * change_imag, axis=0),
            jnp.sum(object_real * change_imag - object_imag * change_real, axis=0),
        ],
        axis=1,
    )
    weight = jnp.sum(patches * patches, axis=(0, 1))
    return (object_gradient, probe_gradient, weight)


def shards(object_amplitude, object_phase, probe, amplitudes, positions):
    tile_side = object_amplitude.shape[0]
    frame_side = probe.shape[2]
    frame_count = amplitudes.shape[0]
    object_field = jnp.stack(
        [object_amplitude * jnp.cos(object_phase), object_amplitude * jnp.sin(object_phase)]
    )
    extended = extended_2(object_field, (("row", 1), ("col", 2)), H)
    starts = positions + H
    patches = jax.vmap(
        lambda start_pair: lax.dynamic_slice(
            extended, (jnp.int32(0), start_pair[0], start_pair[1]), (2, frame_side, frame_side)
        )
    )(starts)
    forward = fourier_table(frame_side, -1.0)
    inverse = fourier_table(frame_side, 1.0)
    object_gradient, probe_gradient, weight = frame_terms(
        patches, probe, amplitudes, forward, inverse
    )
    canvas_side = tile_side + 2 * H

    def place_frame(counter, canvas):
        corner = starts[counter]
        current = lax.dynamic_slice(
            canvas, (jnp.int32(0), corner[0], corner[1]), (2, frame_side, frame_side)
        )
        return lax.dynamic_update_slice(
            canvas, current + object_gradient[counter], (jnp.int32(0), corner[0], corner[1])
        )

    canvas = lax.fori_loop(
        0, frame_count, place_frame, jnp.zeros((2, canvas_side, canvas_side), jnp.float32)
    )
    row_edges = jnp.concatenate([canvas[:, :H], canvas[:, tile_side + H :]], axis=1)
    from_rows = extended_2(row_edges, (("row", 1),), H)
    canvas = canvas.at[:, H : 2 * H].add(from_rows[:, :H])
    canvas = canvas.at[:, tile_side : tile_side + H].add(from_rows[:, 3 * H :])
    middle = canvas[:, H : tile_side + H]
    col_edges = jnp.concatenate([middle[:, :, :H], middle[:, :, tile_side + H :]], axis=2)
    from_cols = extended_2(col_edges, (("col", 2),), H)
    inner = middle[:, :, H : tile_side + H]
    inner = inner.at[:, :, :H].add(from_cols[:, :, :H])
    inner = inner.at[:, :, tile_side - H :].add(from_cols[:, :, 3 * H :])
    step_size = 1.0 / (jnp.max(jnp.sum(probe * probe, axis=(0, 1))) + 1e-06)
    new_object = object_field + inner * step_size
    total_gradient, total_weight = lax.psum((probe_gradient, weight), ("row", "col"))
    new_probe = probe + total_gradient / (total_weight + 1e-05)
    return (new_object, new_probe)


def solution(mesh):
    in_specs = (
        P("row", "col"),
        P("row", "col"),
        P(),
        P(("row", "col"), None, None),
        P(("row", "col"), None),
    )
    out_specs = (P(None, "row", "col"), P())
    return jax.shard_map(shards, mesh=mesh, in_specs=in_specs, out_specs=out_specs, check_vma=False)
```

profile of v0, /device:TPU:0, one launch (start us, length us, event | category | flops | bytes accessed | tf_op | source)
XLA Modules:
  0.0 420.4 jit_solution(17351413524869489684)
XLA Ops:
  7.2 1.9 multiply_bitcast_fusion.1
  9.9 5.0 %collective-permute-start = (f32[2,64,256]{2,1,0:T(8,128)}, f32[2,64,256]{2,1,0:T(8,128)S(1)}, u32[]{:S(2)}, u32[]{:S(2)}) collective-permute-start(f32[2,64,256]{2,1,0:T(8,128)} %get-tuple-element.196), channel_id=1, source_target_pairs={{0,8},{8,16},{16,24},{1,9},{9,17},{17,25},{2,10},{10,18},{18,26},{... | collective-permute-start | bytes 393224 | tf_op jit(solution)/shard_map/ppermute | solution.py:15
  14.9 1.3 collective-permute-start.1
  16.2 1.1 multiply_convert_fusion
  18.0 2.7 slice_bitcast_fusion.5
  21.7 2.9 copy.52
  24.6 1.6 copy.46
  26.1 1.3 copy.49
  28.7 1.5 collective-permute-start.2
  30.2 1.5 collective-permute-start.3
  31.7 1.0 fusion.28
  32.8 2.6 collective-permute-done.3
  35.9 24.2 %while.19 = (s32[]{:T(128)}, f32[2,384,384]{2,1,0:T(8,128)S(1)}, s32[8,3]{0,1:T(4,128)S(1)}, f32[8,2,256,256]{3,2,1,0:T(8,128)}, s32[]{:T(128)}) while((s32[]{:T(128)}, f32[2,384,384]{2,1,0:T(8,128)S(1)}, s32[8,3]{0,1:T(4,128)S(1)}, f32[8,2,256,256]{3,2,1,0:T(8,128)}, s32[]{:T(128)}) %tuple.90), condition=%wide.while_cond.4, body=%wide.while_body.4.sunk | while | flops 2 | bytes 1049717 | solution.py:93
  36.6 2.4 bitcast_dynamic-update-slice_fusion.2
  39.6 2.4 bitcast_dynamic-update-slice_fusion.2
  42.6 2.4 bitcast_dynamic-update-slice_fusion.2
  45.7 2.3 bitcast_dynamic-update-slice_fusion.2
  48.7 2.4 bitcast_dynamic-update-slice_fusion.2
  51.7 2.3 bitcast_dynamic-update-slice_fusion.2
  54.7 2.3 bitcast_dynamic-update-slice_fusion.2
  57.7 2.3 bitcast_dynamic-update-slice_fusion.2
  60.1 4.7 %slice_bitcast_fusion.3 = (f32[8,256,256]{2,1,0:T(8,128)}, f32[8,256,256]{2,1,0:T(8,128)}) fusion(f32[8,2,256,256]{3,2,1,0:T(8,128)} %get-tuple-element.137), kind=kLoop, calls=%fused_computation.35 | loop fusion | bytes 8388608 | tf_op jit(solution)/shard_map/mul | solution.py:52
  64.7 1.9 copy.48
  66.7 2.9 copy.50
  69.6 8.3 %multiply_subtract_fusion = (f32[8,4,1,256,256]{3,4,2,1,0:T(8,128)}, f32[8,4,1,256,256]{3,4,2,1,0:T(8,128)}) fusion(f32[8,256,256]{1,2,0:T(8,128)} %copy.50, f32[4,256,256]{1,2,0:T(8,128)} %copy.49, f32[8,256,256]{1,2,0:T(8,128)S(1)} %copy.48, f32[4,256,256]{1,2,0:T(8,128)S(1)} %copy.46), kind=kLoop, calls=%fused_computation.27 | loop fusion | flops 12582912 | bytes 23068672 | tf_op jit(solution)/shard_map/sub | solution.py:52
  77.8 19.9 %fusion = (f32[8,256,256]{1,2,0:T(8,128)}, f32[2,256,8,4,256,1]{4,1,5,3,2,0:T(8,128)}) fusion(f32[8,4,1,256,256]{3,4,2,1,0:T(8,128)} %get-tuple-element.185, f32[8,4,1,256,256]{3,4,2,1,0:T(8,128)} %get-tuple-element.184, bf16[1,256,2,256]{3,1,2,0:T(8,128)(2,1)} %get-tuple-element.201, bf16[1,256,2,256]{3,1,2,0:T(8,128)(2,1)} %get-tuple-element.202), kind=kOutput, calls=%fused_computation.10 | convolution fusion | flops 8620867584 | bytes 36175872 | tf_op jit(solution)/shard_map/fmakx,blax->fmbkl/dot_general | solution.py:37
  97.8 4.2 %maximum_divide_fusion = f32[8,256,256]{1,2,0:T(8,128)} fusion(f32[8,256,256]{1,2,0:T(8,128)} %copy.52, f32[8,256,256]{1,2,0:T(8,128)} %get-tuple-element.206), kind=kLoop, calls=%fused_computation.33 | loop fusion | flops 1048576 | bytes 6291456 | tf_op jit(solution)/shard_map/div | solution.py:59
  102.0 22.2 %bitcast_subtract_fusion = f32[8,4,2,256,256]{3,4,2,1,0:T(8,128)} fusion(f32[8,4,1,256,256]{3,4,2,1,0:T(8,128)} %get-tuple-element.185, f32[8,4,1,256,256]{3,4,2,1,0:T(8,128)} %get-tuple-element.184, bf16[1,256,2,256]{3,1,2,0:T(8,128)(2,1)} %get-tuple-element.203, bf16[1,256,2,256]{3,1,2,0:T(8,128)(2,1)} %get-tuple-element.200, ...), kind=kOutput, calls=%fused_computation.6 | convolution fusion | flops 8613003264 | bytes 52953088 | tf_op jit(solution)/shard_map/fmakx,blax->fmbkl/dot_general | solution.py:37
  124.2 11.0 %add_reduce_fusion = (f32[4,256,256]{1,2,0:T(8,128)}, f32[4,256,256]{1,2,0:T(8,128)}, f32[8,256,256]{1,2,0:T(8,128)S(1)}, f32[8,256,256]{1,2,0:T(8,128)S(1)}) fusion(f32[8,4,2,256,256]{3,4,2,1,0:T(8,128)} %bitcast_subtract_fusion, f32[8,256,256]{1,2,0:T(8,128)} %copy.50, f32[8,256,256]{1,2,0:T(8,128)S(1)} %copy.48, f32[4,256,256]{1,2,0:T(8,128)} %copy.49, ...), kind=kLoop, calls=%fused_computation.23 | loop fusion | flops 31981568 | bytes 29360128 | tf_op jit(solution)/shard_map/reduce_sum | solution.py:74
  135.2 2.2 pad_maximum_fusion.1
  137.5 108.3 %while.18 = (s32[]{:T(128)}, f32[2,384,384]{2,1,0:T(8,128)S(1)}, s32[8,2]{0,1:T(2,128)S(1)}, f32[8,2,256,256]{2,3,0,1:T(8,128)}, s32[]{:T(128)}, /*index=5*/s32[]{:T(128)}, s32[]{:T(128)}) while((s32[]{:T(128)}, f32[2,384,384]{2,1,0:T(8,128)S(1)}, s32[8,2]{0,1:T(2,128)S(1)}, f32[8,2,256,256]{2,3,0,1:T(8,128)}, s32[]{:T(128)}, ...), condition=%wide.region_4.5_spmd, body=%wide.region_3.4_spmd.sunk | while | flops 131080 | bytes 4718797 | solution.py:113
  142.0 1.1 constant_dynamic-slice_fusion.6
  143.5 7.7 %dynamic_update_slice.8 = f32[2,384,384]{2,1,0:T(8,128)S(1)} dynamic-update-slice(f32[2,384,384]{2,1,0:T(8,128)S(1)} %get-tuple-element.293, f32[2,256,256]{2,1,0:T(8,128)S(1)} %bitcast_add_fusion.2, s32[]{:T(128)} %constant.166.clone.1..sunk, s32[]{:T(128)S(6)} %select_n.100, s32[]{:T(128)S(6)} %select_n.101) | dynamic-update-slice | bytes 1048580 | tf_op jit(solution)/shard_map/while/body/eval_jaxpr/dynamic_update_slice | solution.py:109
  155.7 1.1 constant_dynamic-slice_fusion.6
  157.2 7.9 %dynamic_update_slice.8 = f32[2,384,384]{2,1,0:T(8,128)S(1)} dynamic-update-slice(f32[2,384,384]{2,1,0:T(8,128)S(1)} %get-tuple-element.293, f32[2,256,256]{2,1,0:T(8,128)S(1)} %bitcast_add_fusion.2, s32[]{:T(128)} %constant.166.clone.1..sunk, s32[]{:T(128)S(6)} %select_n.100, s32[]{:T(128)S(6)} %select_n.101) | dynamic-update-slice | bytes 1048580 | tf_op jit(solution)/shard_map/while/body/eval_jaxpr/dynamic_update_slice | solution.py:109
  169.6 1.1 constant_dynamic-slice_fusion.6
  171.1 7.9 %dynamic_update_slice.8 = f32[2,384,384]{2,1,0:T(8,128)S(1)} dynamic-update-slice(f32[2,384,384]{2,1,0:T(8,128)S(1)} %get-tuple-element.293, f32[2,256,256]{2,1,0:T(8,128)S(1)} %bitcast_add_fusion.2, s32[]{:T(128)} %constant.166.clone.1..sunk, s32[]{:T(128)S(6)} %select_n.100, s32[]{:T(128)S(6)} %select_n.101) | dynamic-update-slice | bytes 1048580 | tf_op jit(solution)/shard_map/while/body/eval_jaxpr/dynamic_update_slice | solution.py:109
  183.5 1.1 constant_dynamic-slice_fusion.6
  185.0 7.7 %dynamic_update_slice.8 = f32[2,384,384]{2,1,0:T(8,128)S(1)} dynamic-update-slice(f32[2,384,384]{2,1,0:T(8,128)S(1)} %get-tuple-element.293, f32[2,256,256]{2,1,0:T(8,128)S(1)} %bitcast_add_fusion.2, s32[]{:T(128)} %constant.166.clone.1..sunk, s32[]{:T(128)S(6)} %select_n.100, s32[]{:T(128)S(6)} %select_n.101) | dynamic-update-slice | bytes 1048580 | tf_op jit(solution)/shard_map/while/body/eval_jaxpr/dynamic_update_slice | solution.py:109
  197.3 1.1 constant_dynamic-slice_fusion.6
  198.8 7.5 %dynamic_update_slice.8 = f32[2,384,384]{2,1,0:T(8,128)S(1)} dynamic-update-slice(f32[2,384,384]{2,1,0:T(8,128)S(1)} %get-tuple-element.293, f32[2,256,256]{2,1,0:T(8,128)S(1)} %bitcast_add_fusion.2, s32[]{:T(128)} %constant.166.clone.1..sunk, s32[]{:T(128)S(6)} %select_n.100, s32[]{:T(128)S(6)} %select_n.101) | dynamic-update-slice | bytes 1048580 | tf_op jit(solution)/shard_map/while/body/eval_jaxpr/dynamic_update_slice | solution.py:109
  210.8 1.1 constant_dynamic-slice_fusion.6
  212.3 7.1 %dynamic_update_slice.8 = f32[2,384,384]{2,1,0:T(8,128)S(1)} dynamic-update-slice(f32[2,384,384]{2,1,0:T(8,128)S(1)} %get-tuple-element.293, f32[2,256,256]{2,1,0:T(8,128)S(1)} %bitcast_add_fusion.2, s32[]{:T(128)} %constant.166.clone.1..sunk, s32[]{:T(128)S(6)} %select_n.100, s32[]{:T(128)S(6)} %select_n.101) | dynamic-update-slice | bytes 1048580 | tf_op jit(solution)/shard_map/while/body/eval_jaxpr/dynamic_update_slice | solution.py:109
  223.9 1.1 constant_dynamic-slice_fusion.6
  225.4 6.9 %dynamic_update_slice.8 = f32[2,384,384]{2,1,0:T(8,128)S(1)} dynamic-update-slice(f32[2,384,384]{2,1,0:T(8,128)S(1)} %get-tuple-element.293, f32[2,256,256]{2,1,0:T(8,128)S(1)} %bitcast_add_fusion.2, s32[]{:T(128)} %constant.166.clone.1..sunk, s32[]{:T(128)S(6)} %select_n.100, s32[]{:T(128)S(6)} %select_n.101) | dynamic-update-slice | bytes 1048580 | tf_op jit(solution)/shard_map/while/body/eval_jaxpr/dynamic_update_slice | solution.py:109
  236.9 1.1 constant_dynamic-slice_fusion.6
  238.4 7.4 %dynamic_update_slice.8 = f32[2,384,384]{2,1,0:T(8,128)S(1)} dynamic-update-slice(f32[2,384,384]{2,1,0:T(8,128)S(1)} %get-tuple-element.293, f32[2,256,256]{2,1,0:T(8,128)S(1)} %bitcast_add_fusion.2, s32[]{:T(128)} %constant.166.clone.1..sunk, s32[]{:T(128)S(6)} %select_n.100, s32[]{:T(128)S(6)} %select_n.101) | dynamic-update-slice | bytes 1048580 | tf_op jit(solution)/shard_map/while/body/eval_jaxpr/dynamic_update_slice | solution.py:109
  245.8 3.0 collective-permute-start.4
  248.8 2.9 copy.61
  252.7 1.3 collective-permute-start.5
  254.0 3.2 multiply_reduce_fusion
  257.3 3.2 pad_maximum_fusion.2
  260.5 1.6 collective-permute-done.5
  263.9 9.9 %collective-permute-start.6 = (f32[2,256,64]{2,1,0:T(8,128)}, f32[2,256,64]{2,1,0:T(8,128)}, u32[]{:S(2)}, u32[]{:S(2)}) collective-permute-start(f32[2,256,64]{2,1,0:T(8,128)} %get-tuple-element.191), channel_id=1, source_target_pairs={{0,1},{1,2},{2,3},{3,4},{4,5},{5,6},{6,7},{8,9},{9,10},{10,11},{11... | collective-permute-start | bytes 393224 | tf_op jit(solution)/shard_map/ppermute | solution.py:15
  274.7 1.7 reduce_max.9
  277.3 1.3 collective-permute-start.7
  278.7 1.1 slice_add_fusion.1
  279.7 1.1 scatter-add.16
  280.9 1.3 collective-permute-done.7
  282.3 1.2 scatter-add.19
  283.5 1.8 fusion.18
  285.3 122.8 %all-reduce.3.cloned.1.call-done = (f32[4,2,256,256]{2,3,0,1:T(8,128)}, f32[256,256]{1,0:T(8,128)}) async-done(((f32[4,2,256,256]{2,3,0,1:T(8,128)}, f32[256,256]{1,0:T(8,128)}), (f32[4,2,256,256]{2,3,0,1:T(8,128)}, f32[256,256]{1,0:T(8,128)})) %all-reduce.3.cloned.1.call-update) | async-done | bytes 2359312 | tf_op jit(solution)/shard_map/psum | solution.py:128
  409.2 2.6 divide_add_fusion
  411.8 1.8 copy.62
  (80 shorter events, 22.9 us)
Async XLA Ops:
  7.2 400.9 %all-reduce.3.cloned.1.call-start = ((), (), s32[]{:S(2)}) async-start(), calls=%async_computation | async-start | bytes 4718592 | tf_op jit(solution)/shard_map/psum | solution.py:128
  9.2 26.2 %copy-start.1 = (f32[1,256,256]{2,1,0:T(8,128)}, f32[1,256,256]{2,1,0:T(8,128)S(1)}, u32[]{:S(2)}) copy-start(f32[1,256,256]{2,1,0:T(8,128)S(1)} %get-tuple-element.199) | copy-start | bytes 786436
  9.9 18.6 %collective-permute-start = (f32[2,64,256]{2,1,0:T(8,128)}, f32[2,64,256]{2,1,0:T(8,128)S(1)}, u32[]{:S(2)}, u32[]{:S(2)}) collective-permute-start(f32[2,64,256]{2,1,0:T(8,128)} %get-tuple-element.196), channel_id=1, source_target_pairs={{0,8},{8,16},{16,24},{1,9},{9,17},{17,25},{2,10},{10,18},{18,26},{... | collective-permute-start | bytes 393224 | tf_op jit(solution)/shard_map/ppermute | solution.py:15
  14.9 13.6 %collective-permute-start.1 = (f32[2,64,256]{2,1,0:T(8,128)}, f32[2,64,256]{2,1,0:T(8,128)S(1)}, u32[]{:S(2)}, u32[]{:S(2)}) collective-permute-start(f32[2,64,256]{2,1,0:T(8,128)} %get-tuple-element.197), channel_id=1, source_target_pairs={{8,0},{16,8},{24,16},{9,1},{17,9},{25,17},{10,2},{18,10},{26,18},{... | collective-permute-start | bytes 393224 | tf_op jit(solution)/shard_map/ppermute | solution.py:18
  28.7 4.0 collective-permute-start.2
  30.2 5.2 %collective-permute-start.3 = (f32[2,384,64]{2,1,0:T(8,128)S(1)}, f32[2,384,64]{2,1,0:T(8,128)S(1)}, u32[]{:S(2)}, u32[]{:S(2)}) collective-permute-start(f32[2,384,64]{2,1,0:T(8,128)S(1)} %get-tuple-element.195), channel_id=1, source_target_pairs={{1,0},{2,1},{3,2},{4,3},{5,4},{6,5},{7,6},{9,8},{10,9},{11,10},{12... | collective-permute-start | bytes 589832 | tf_op jit(solution)/shard_map/ppermute | solution.py:18
  245.8 6.2 %collective-permute-start.4 = (f32[2,64,384]{2,1,0:T(8,128)S(1)}, f32[2,64,384]{2,1,0:T(8,128)S(1)}, u32[]{:S(2)}, u32[]{:S(2)}) collective-permute-start(f32[2,64,384]{2,1,0:T(8,128)S(1)} %slice.183), channel_id=1, source_target_pairs={{0,8},{8,16},{16,24},{1,9},{9,17},{17,25},{2,10},{10,18},{18,26},{... | collective-permute-start | bytes 589832 | tf_op jit(solution)/shard_map/ppermute | solution.py:15
  252.7 9.3 %collective-permute-start.5 = (f32[2,64,384]{2,1,0:T(8,128)}, f32[2,64,384]{2,1,0:T(8,128)}, u32[]{:S(2)}, u32[]{:S(2)}) collective-permute-start(f32[2,64,384]{2,1,0:T(8,128)} %get-tuple-element.192), channel_id=1, source_target_pairs={{8,0},{16,8},{24,16},{9,1},{17,9},{25,17},{10,2},{18,10},{26,18},{... | collective-permute-start | bytes 589832 | tf_op jit(solution)/shard_map/ppermute | solution.py:18
  257.3 16.6 %copy-start = (f32[4,2,256,256]{3,2,1,0:T(8,128)S(1)}, f32[4,2,256,256]{3,2,1,0:T(8,128)}, u32[]{:S(2)}) copy-start(f32[4,2,256,256]{3,2,1,0:T(8,128)} %param.17) | copy-start | bytes 6291460
  263.9 14.7 %collective-permute-start.6 = (f32[2,256,64]{2,1,0:T(8,128)}, f32[2,256,64]{2,1,0:T(8,128)}, u32[]{:S(2)}, u32[]{:S(2)}) collective-permute-start(f32[2,256,64]{2,1,0:T(8,128)} %get-tuple-element.191), channel_id=1, source_target_pairs={{0,1},{1,2},{2,3},{3,4},{4,5},{5,6},{6,7},{8,9},{9,10},{10,11},{11... | collective-permute-start | bytes 393224 | tf_op jit(solution)/shard_map/ppermute | solution.py:15
  277.3 4.8 %collective-permute-start.7 = (f32[2,256,64]{2,1,0:T(8,128)}, f32[2,256,64]{2,1,0:T(8,128)S(1)}, u32[]{:S(2)}, u32[]{:S(2)}) collective-permute-start(f32[2,256,64]{2,1,0:T(8,128)} %get-tuple-element.190), channel_id=1, source_target_pairs={{1,0},{2,1},{3,2},{4,3},{5,4},{6,5},{7,6},{9,8},{10,9},{11,10},{12... | collective-permute-start | bytes 393224 | tf_op jit(solution)/shard_map/ppermute | solution.py:18
Sparse Core Ops, SparseCore 0:
  260.6 147.4 all-reduce.2
where the time goes:
time: 422 us; the launch traced here: 420 us
  waiting for transfers between devices  129 us (31%)
  local copies, waits for them, and re-layouts  126 us (30%)
  other arithmetic  52.8 us (13%)
  matrix products  42.1 us (10%)
  loops' own time  31.4 us (7%)
  starting transfers between devices  24.7 us (6%)
  between operations  15 us (4%)
    psum x1, waiting for transfers between devices, shards(): lax.psum((probe_gradient, weight), ('row', 'col'))  123 us
    dynamic_update_slice x8, local copies, waits for them, and re-layouts, place_frame(): lax.dynamic_update_slice(canvas, current + object_gradient[counter], (jnp...  60.1 us
    dot_general x2, matrix products, transform(): jnp.einsum('fmakx,blax->fmbkl', halfway.astype(jnp.bfloat16), matrix, pre...  42.1 us
    another operation x1, loops' own time, shards(): lax.fori_loop(0, frame_count, place_frame, jnp.zeros((2, canvas_side, can...  31.4 us
    gather x24, local copies, waits for them, and re-layouts  24.2 us
    ppermute x4, starting transfers between devices, extended_2(): lax.ppermute(lax.slice_in_dim(block, block.shape[dim] - width, None, axis...  19.4 us
    reduce_sum x1, other arithmetic, frame_terms(): jnp.sum(object_real * change_real + object_imag * change_imag, axis=0)  11 us
    dynamic_slice x16, local copies, waits for them, and re-layouts, place_frame(): object_gradient[counter]  10.3 us
  transfers between devices with their start and end apart: 9, of which 5 were waited for; matrix products, arithmetic and copies ran while one was open for 8% of the time, Pallas kernels for 0%

commit v1 on v0

--- a/solution.py
+++ b/solution.py
@@ -125,7 +125,7 @@
     inner = inner.at[:, :, tile_side - H :].add(from_cols[:, :, 3 * H :])
     step_size = 1.0 / (jnp.max(jnp.sum(probe * probe, axis=(0, 1))) + 1e-06)
     new_object = object_field + inner * step_size
-    total_gradient, total_weight = lax.psum((probe_gradient, weight), ("row", "col"))
+    total_gradient, total_weight = lax.psum(lax.psum((probe_gradient, weight), "col"), "row")
     new_probe = probe + total_gradient / (total_weight + 1e-05)
     return (new_object, new_probe)
 

time: 422 us -> 372 us (0.88); the launches traced: 420 us -> 366 us
  waiting for transfers between devices: 129 us -> 82.3 us
  starting transfers between devices: 24.7 us -> 15.9 us
    psum x1 -> x2, waiting for transfers between devices: 123 us -> 66.8 us  [the longest x1 66.8 us: shards(): lax.psum((probe_gradient, weight), 'col')]
    ppermute x4, starting transfers between devices: 19.4 us -> 10.4 us  [extended_2(): lax.ppermute(lax.slice_in_dim(block, block.shape[dim] - width, None, axis...]
    ppermute x4, waiting for transfers between devices: 0.27 us -> 5.17 us  [extended_2(): lax.ppermute(lax.slice_in_dim(block, block.shape[dim] - width, None, axis...]
    ppermute x4, waiting for transfers between devices: 5.53 us -> 10.3 us  [extended_2(): lax.ppermute(lax.slice_in_dim(block, 0, width, axis=dim), axis, backward)]
    unnamed x7 -> x11, local copies, waits for them, and re-layouts: 7.59 us -> 8.54 us
  transfers between devices with their start and end apart: 9 -> 10, of which waited for: 5 -> 5; matrix products, arithmetic and copies ran while one was open for 8% -> 30% of each run, Pallas kernels for 0% -> 0%
where the time goes in v1:
time: 372 us; the launch traced here: 366 us
  local copies, waits for them, and re-layouts  125 us (34%)
  waiting for transfers between devices  82.3 us (22%)
  other arithmetic  53.7 us (14%)
  matrix products  42 us (11%)
  loops' own time  32.5 us (9%)
  starting transfers between devices  15.9 us (4%)
  between operations  15 us (4%)
    psum x1, waiting for transfers between devices, shards(): lax.psum((probe_gradient, weight), 'col')  66.8 us
    dynamic_update_slice x8, local copies, waits for them, and re-layouts, place_frame(): lax.dynamic_update_slice(canvas, current + object_gradient[counter], (jnp...  60.1 us
    dot_general x2, matrix products, transform(): jnp.einsum('fmakx,blax->fmbkl', halfway.astype(jnp.bfloat16), matrix, pre...  42 us
    another operation x1, loops' own time, shards(): lax.fori_loop(0, frame_count, place_frame, jnp.zeros((2, canvas_side, can...  32.5 us
    gather x24, local copies, waits for them, and re-layouts  23.9 us
    reduce_sum x1, other arithmetic, frame_terms(): jnp.sum(object_real * change_real + object_imag * change_imag, axis=0)  11.7 us
    ppermute x4, starting transfers between devices, extended_2(): lax.ppermute(lax.slice_in_dim(block, block.shape[dim] - width, None, axis...  10.4 us
    ppermute x4, waiting for transfers between devices, extended_2(): lax.ppermute(lax.slice_in_dim(block, 0, width, axis=dim), axis, backward)  10.3 us
  transfers between devices with their start and end apart: 10, of which 5 were waited for; matrix products, arithmetic and copies ran while one was open for 30% of the time, Pallas kernels for 0%

profile of v1, /device:TPU:0, one launch (start us, length us, event | category | flops | bytes accessed | tf_op | source)
XLA Modules:
  0.0 366.2 jit_solution(12663642508217772208)
XLA Ops:
  7.2 1.9 multiply_bitcast_fusion.1
  10.0 5.0 %collective-permute-start = (f32[2,64,256]{2,1,0:T(8,128)}, f32[2,64,256]{2,1,0:T(8,128)S(1)}, u32[]{:S(2)}, u32[]{:S(2)}) collective-permute-start(f32[2,64,256]{2,1,0:T(8,128)} %get-tuple-element.198), channel_id=1, source_target_pairs={{0,8},{8,16},{16,24},{1,9},{9,17},{17,25},{2,10},{10,18},{18,26},{... | collective-permute-start | bytes 393224 | tf_op jit(solution)/shard_map/ppermute | solution.py:15
  14.9 1.3 collective-permute-start.1
  16.2 1.1 multiply_convert_fusion
  18.0 2.7 slice_bitcast_fusion.5
  21.7 2.9 copy.52
  24.7 1.6 copy.46
  26.2 1.3 copy.49
  28.8 1.5 collective-permute-start.2
  30.3 1.5 collective-permute-start.3
  32.8 2.6 collective-permute-done.3
  35.9 23.9 %while.19 = (s32[]{:T(128)}, f32[2,384,384]{2,1,0:T(8,128)S(1)}, s32[8,3]{0,1:T(4,128)S(1)}, f32[8,2,256,256]{3,2,1,0:T(8,128)}, s32[]{:T(128)}) while((s32[]{:T(128)}, f32[2,384,384]{2,1,0:T(8,128)S(1)}, s32[8,3]{0,1:T(4,128)S(1)}, f32[8,2,256,256]{3,2,1,0:T(8,128)}, s32[]{:T(128)}) %tuple.90), condition=%wide.while_cond.4, body=%wide.while_body.4.sunk | while | flops 2 | bytes 1049717 | solution.py:93
  36.6 2.3 bitcast_dynamic-update-slice_fusion.2
  39.6 2.3 bitcast_dynamic-update-slice_fusion.2
  42.6 2.4 bitcast_dynamic-update-slice_fusion.2
  45.6 2.3 bitcast_dynamic-update-slice_fusion.2
  48.6 2.3 bitcast_dynamic-update-slice_fusion.2
  51.6 2.3 bitcast_dynamic-update-slice_fusion.2
  54.6 2.3 bitcast_dynamic-update-slice_fusion.2
  57.5 2.3 bitcast_dynamic-update-slice_fusion.2
  59.9 3.4 multiply_reduce_fusion
  63.3 2.4 slice_bitcast_fusion.3
  65.8 1.9 copy.48
  67.7 2.9 copy.50
  70.6 8.3 %multiply_subtract_fusion = (f32[8,4,1,256,256]{3,4,2,1,0:T(8,128)}, f32[8,4,1,256,256]{3,4,2,1,0:T(8,128)}) fusion(f32[8,256,256]{1,2,0:T(8,128)} %copy.50, f32[4,256,256]{1,2,0:T(8,128)} %copy.49, f32[8,256,256]{1,2,0:T(8,128)S(1)} %copy.48, f32[4,256,256]{1,2,0:T(8,128)S(1)} %copy.46), kind=kLoop, calls=%fused_computation.27 | loop fusion | flops 12582912 | bytes 23068672 | tf_op jit(solution)/shard_map/sub | solution.py:52
  78.9 19.8 %fusion = (f32[8,256,256]{1,2,0:T(8,128)}, f32[2,256,8,4,256,1]{4,1,5,3,2,0:T(8,128)}) fusion(f32[8,4,1,256,256]{3,4,2,1,0:T(8,128)} %get-tuple-element.187, f32[8,4,1,256,256]{3,4,2,1,0:T(8,128)} %get-tuple-element.186, bf16[1,256,2,256]{3,1,2,0:T(8,128)(2,1)} %get-tuple-element.203, bf16[1,256,2,256]{3,1,2,0:T(8,128)(2,1)} %get-tuple-element.204), kind=kOutput, calls=%fused_computation.10 | convolution fusion | flops 8620867584 | bytes 36175872 | tf_op jit(solution)/shard_map/fmakx,blax->fmbkl/dot_general | solution.py:37
  98.7 4.3 %maximum_divide_fusion = f32[8,256,256]{1,2,0:T(8,128)} fusion(f32[8,256,256]{1,2,0:T(8,128)} %copy.52, f32[8,256,256]{1,2,0:T(8,128)} %get-tuple-element.208), kind=kLoop, calls=%fused_computation.33 | loop fusion | flops 1048576 | bytes 6291456 | tf_op jit(solution)/shard_map/div | solution.py:59
  103.0 22.2 %bitcast_subtract_fusion = f32[8,4,2,256,256]{3,4,2,1,0:T(8,128)} fusion(f32[8,4,1,256,256]{3,4,2,1,0:T(8,128)} %get-tuple-element.187, f32[8,4,1,256,256]{3,4,2,1,0:T(8,128)} %get-tuple-element.186, bf16[1,256,2,256]{3,1,2,0:T(8,128)(2,1)} %get-tuple-element.205, bf16[1,256,2,256]{3,1,2,0:T(8,128)(2,1)} %get-tuple-element.202, ...), kind=kOutput, calls=%fused_computation.6 | convolution fusion | flops 8613003264 | bytes 52953088 | tf_op jit(solution)/shard_map/fmakx,blax->fmbkl/dot_general | solution.py:37
  125.2 11.7 %add_reduce_fusion = (f32[4,256,256]{1,2,0:T(8,128)S(1)}, f32[4,256,256]{1,2,0:T(8,128)S(1)}, f32[8,256,256]{1,2,0:T(8,128)}, f32[8,256,256]{1,2,0:T(8,128)}) fusion(f32[8,4,2,256,256]{3,4,2,1,0:T(8,128)} %bitcast_subtract_fusion, f32[8,256,256]{1,2,0:T(8,128)} %copy.50, f32[8,256,256]{1,2,0:T(8,128)S(1)} %copy.48, f32[4,256,256]{1,2,0:T(8,128)} %copy.49, ...), kind=kLoop, calls=%fused_computation.23 | loop fusion | flops 31981568 | bytes 29360128 | tf_op jit(solution)/shard_map/reduce_sum | solution.py:74
  136.9 1.5 pad_maximum_fusion.2
  139.3 3.9 %pad_maximum_fusion.1 = f32[8,2,256,256]{2,3,0,1:T(8,128)} fusion(f32[8,1,256,256]{2,3,0,1:T(8,128)S(1)} %bitcast.152, f32[8,1,256,256]{2,3,0,1:T(8,128)} %bitcast.153), kind=kLoop, calls=%fused_computation.28 | loop fusion | flops 1048576 | bytes 8388608 | tf_op jit(solution)/shard_map/stack | solution.py:65
  143.2 66.8 %all-reduce.5.cloned.1.call-done = (f32[4,2,256,256]{2,3,0,1:T(8,128)}, f32[256,256]{1,0:T(8,128)}) async-done(((f32[4,2,256,256]{2,3,0,1:T(8,128)}, f32[256,256]{1,0:T(8,128)}), (f32[4,2,256,256]{2,3,0,1:T(8,128)}, f32[256,256]{1,0:T(8,128)})) %all-reduce.5.cloned.1.call-update) | async-done | bytes 2359312 | tf_op jit(solution)/shard_map/psum | solution.py:128
  210.1 110.0 %while.18 = (s32[]{:T(128)}, f32[2,384,384]{2,1,0:T(8,128)S(1)}, s32[8,2]{0,1:T(2,128)S(1)}, f32[8,2,256,256]{2,3,0,1:T(8,128)}, s32[]{:T(128)}, /*index=5*/s32[]{:T(128)}, s32[]{:T(128)}) while((s32[]{:T(128)}, f32[2,384,384]{2,1,0:T(8,128)S(1)}, s32[8,2]{0,1:T(2,128)S(1)}, f32[8,2,256,256]{2,3,0,1:T(8,128)}, s32[]{:T(128)}, ...), condition=%wide.region_4.5_spmd, body=%wide.region_3.4_spmd.sunk | while | flops 131080 | bytes 4718797 | solution.py:113
  214.8 1.1 constant_dynamic-slice_fusion.6
  216.4 7.7 %dynamic_update_slice.8 = f32[2,384,384]{2,1,0:T(8,128)S(1)} dynamic-update-slice(f32[2,384,384]{2,1,0:T(8,128)S(1)} %get-tuple-element.295, f32[2,256,256]{2,1,0:T(8,128)S(1)} %bitcast_add_fusion.2, s32[]{:T(128)} %constant.166.clone.1..sunk, s32[]{:T(128)S(6)} %select_n.100, s32[]{:T(128)S(6)} %select_n.101) | dynamic-update-slice | bytes 1048580 | tf_op jit(solution)/shard_map/while/body/eval_jaxpr/dynamic_update_slice | solution.py:109
  228.7 1.1 constant_dynamic-slice_fusion.6
  230.2 7.9 %dynamic_update_slice.8 = f32[2,384,384]{2,1,0:T(8,128)S(1)} dynamic-update-slice(f32[2,384,384]{2,1,0:T(8,128)S(1)} %get-tuple-element.295, f32[2,256,256]{2,1,0:T(8,128)S(1)} %bitcast_add_fusion.2, s32[]{:T(128)} %constant.166.clone.1..sunk, s32[]{:T(128)S(6)} %select_n.100, s32[]{:T(128)S(6)} %select_n.101) | dynamic-update-slice | bytes 1048580 | tf_op jit(solution)/shard_map/while/body/eval_jaxpr/dynamic_update_slice | solution.py:109
  242.9 1.1 constant_dynamic-slice_fusion.6
  244.4 7.9 %dynamic_update_slice.8 = f32[2,384,384]{2,1,0:T(8,128)S(1)} dynamic-update-slice(f32[2,384,384]{2,1,0:T(8,128)S(1)} %get-tuple-element.295, f32[2,256,256]{2,1,0:T(8,128)S(1)} %bitcast_add_fusion.2, s32[]{:T(128)} %constant.166.clone.1..sunk, s32[]{:T(128)S(6)} %select_n.100, s32[]{:T(128)S(6)} %select_n.101) | dynamic-update-slice | bytes 1048580 | tf_op jit(solution)/shard_map/while/body/eval_jaxpr/dynamic_update_slice | solution.py:109
  257.0 1.1 constant_dynamic-slice_fusion.6
  258.5 7.7 %dynamic_update_slice.8 = f32[2,384,384]{2,1,0:T(8,128)S(1)} dynamic-update-slice(f32[2,384,384]{2,1,0:T(8,128)S(1)} %get-tuple-element.295, f32[2,256,256]{2,1,0:T(8,128)S(1)} %bitcast_add_fusion.2, s32[]{:T(128)} %constant.166.clone.1..sunk, s32[]{:T(128)S(6)} %select_n.100, s32[]{:T(128)S(6)} %select_n.101) | dynamic-update-slice | bytes 1048580 | tf_op jit(solution)/shard_map/while/body/eval_jaxpr/dynamic_update_slice | solution.py:109
  271.0 1.1 constant_dynamic-slice_fusion.6
  272.5 7.5 %dynamic_update_slice.8 = f32[2,384,384]{2,1,0:T(8,128)S(1)} dynamic-update-slice(f32[2,384,384]{2,1,0:T(8,128)S(1)} %get-tuple-element.295, f32[2,256,256]{2,1,0:T(8,128)S(1)} %bitcast_add_fusion.2, s32[]{:T(128)} %constant.166.clone.1..sunk, s32[]{:T(128)S(6)} %select_n.100, s32[]{:T(128)S(6)} %select_n.101) | dynamic-update-slice | bytes 1048580 | tf_op jit(solution)/shard_map/while/body/eval_jaxpr/dynamic_update_slice | solution.py:109
  284.7 1.1 constant_dynamic-slice_fusion.6
  286.2 7.1 %dynamic_update_slice.8 = f32[2,384,384]{2,1,0:T(8,128)S(1)} dynamic-update-slice(f32[2,384,384]{2,1,0:T(8,128)S(1)} %get-tuple-element.295, f32[2,256,256]{2,1,0:T(8,128)S(1)} %bitcast_add_fusion.2, s32[]{:T(128)} %constant.166.clone.1..sunk, s32[]{:T(128)S(6)} %select_n.100, s32[]{:T(128)S(6)} %select_n.101) | dynamic-update-slice | bytes 1048580 | tf_op jit(solution)/shard_map/while/body/eval_jaxpr/dynamic_update_slice | solution.py:109
  298.0 1.1 constant_dynamic-slice_fusion.6
  299.5 6.9 %dynamic_update_slice.8 = f32[2,384,384]{2,1,0:T(8,128)S(1)} dynamic-update-slice(f32[2,384,384]{2,1,0:T(8,128)S(1)} %get-tuple-element.295, f32[2,256,256]{2,1,0:T(8,128)S(1)} %bitcast_add_fusion.2, s32[]{:T(128)} %constant.166.clone.1..sunk, s32[]{:T(128)S(6)} %select_n.100, s32[]{:T(128)S(6)} %select_n.101) | dynamic-update-slice | bytes 1048580 | tf_op jit(solution)/shard_map/while/body/eval_jaxpr/dynamic_update_slice | solution.py:109
  311.2 1.1 constant_dynamic-slice_fusion.6
  312.7 7.4 %dynamic_update_slice.8 = f32[2,384,384]{2,1,0:T(8,128)S(1)} dynamic-update-slice(f32[2,384,384]{2,1,0:T(8,128)S(1)} %get-tuple-element.295, f32[2,256,256]{2,1,0:T(8,128)S(1)} %bitcast_add_fusion.2, s32[]{:T(128)} %constant.166.clone.1..sunk, s32[]{:T(128)S(6)} %select_n.100, s32[]{:T(128)S(6)} %select_n.101) | dynamic-update-slice | bytes 1048580 | tf_op jit(solution)/shard_map/while/body/eval_jaxpr/dynamic_update_slice | solution.py:109
  320.2 2.0 collective-permute-start.4
  322.2 5.2 %collective-permute-done.4 = f32[2,64,384]{2,1,0:T(8,128)S(1)} collective-permute-done((f32[2,64,384]{2,1,0:T(8,128)S(1)}, f32[2,64,384]{2,1,0:T(8,128)S(1)}, u32[]{:S(2)}, u32[]{:S(2)}) %collective-permute-start.4) | collective-permute-done | bytes 196640 | tf_op jit(solution)/shard_map/ppermute | solution.py:15
  328.1 1.3 collective-permute-start.5
  329.4 2.9 copy.61
  332.3 5.6 %collective-permute-done.5 = f32[2,64,384]{2,1,0:T(8,128)} collective-permute-done((f32[2,64,384]{2,1,0:T(8,128)}, f32[2,64,384]{2,1,0:T(8,128)}, u32[]{:S(2)}, u32[]{:S(2)}) %collective-permute-start.5) | collective-permute-done | bytes 196640 | tf_op jit(solution)/shard_map/ppermute | solution.py:18
  339.7 2.0 collective-permute-start.6
  342.6 1.6 reduce_max.9
  345.1 1.3 collective-permute-start.7
  346.4 1.1 slice_add_fusion.1
  347.5 1.1 scatter-add.16
  348.6 2.1 collective-permute-done.7
  350.8 1.2 scatter-add.19
  352.0 1.8 fusion.18
  355.0 2.6 divide_add_fusion
  357.5 1.8 copy.62
  (87 shorter events, 25.1 us)
Async XLA Ops:
  7.2 202.9 %all-reduce.5.cloned.1.call-start = ((), (), s32[]{:S(2)}) async-start(), calls=%async_computation | async-start | bytes 4718592 | tf_op jit(solution)/shard_map/psum | solution.py:128
  9.2 26.3 %copy-start.3 = (f32[1,256,256]{2,1,0:T(8,128)}, f32[1,256,256]{2,1,0:T(8,128)S(1)}, u32[]{:S(2)}) copy-start(f32[1,256,256]{2,1,0:T(8,128)S(1)} %get-tuple-element.201) | copy-start | bytes 786436
  10.0 18.6 %collective-permute-start = (f32[2,64,256]{2,1,0:T(8,128)}, f32[2,64,256]{2,1,0:T(8,128)S(1)}, u32[]{:S(2)}, u32[]{:S(2)}) collective-permute-start(f32[2,64,256]{2,1,0:T(8,128)} %get-tuple-element.198), channel_id=1, source_target_pairs={{0,8},{8,16},{16,24},{1,9},{9,17},{17,25},{2,10},{10,18},{18,26},{... | collective-permute-start | bytes 393224 | tf_op jit(solution)/shard_map/ppermute | solution.py:15
  14.9 13.6 %collective-permute-start.1 = (f32[2,64,256]{2,1,0:T(8,128)}, f32[2,64,256]{2,1,0:T(8,128)S(1)}, u32[]{:S(2)}, u32[]{:S(2)}) collective-permute-start(f32[2,64,256]{2,1,0:T(8,128)} %get-tuple-element.199), channel_id=1, source_target_pairs={{8,0},{16,8},{24,16},{9,1},{17,9},{25,17},{10,2},{18,10},{26,18},{... | collective-permute-start | bytes 393224 | tf_op jit(solution)/shard_map/ppermute | solution.py:18
  28.8 4.0 %collective-permute-start.2 = (f32[2,384,64]{2,1,0:T(8,128)S(1)}, f32[2,384,64]{2,1,0:T(8,128)S(1)}, u32[]{:S(2)}, u32[]{:S(2)}) collective-permute-start(f32[2,384,64]{2,1,0:T(8,128)S(1)} %get-tuple-element.196), channel_id=1, source_target_pairs={{0,1},{1,2},{2,3},{3,4},{4,5},{5,6},{6,7},{8,9},{9,10},{10,11},{11... | collective-permute-start | bytes 589832 | tf_op jit(solution)/shard_map/ppermute | solution.py:15
  30.3 5.2 %collective-permute-start.3 = (f32[2,384,64]{2,1,0:T(8,128)S(1)}, f32[2,384,64]{2,1,0:T(8,128)S(1)}, u32[]{:S(2)}, u32[]{:S(2)}) collective-permute-start(f32[2,384,64]{2,1,0:T(8,128)S(1)} %get-tuple-element.197), channel_id=1, source_target_pairs={{1,0},{2,1},{3,2},{4,3},{5,4},{6,5},{7,6},{9,8},{10,9},{11,10},{12... | collective-permute-start | bytes 589832 | tf_op jit(solution)/shard_map/ppermute | solution.py:18
  59.9 3.4 copy-start.1
  136.9 2.3 copy-start.2
  138.4 215.4 %all-reduce.7.cloned.1.call-start = ((), (), s32[]{:S(2)}) async-start(), calls=%async_computation.1 | async-start | bytes 4718592 | tf_op jit(solution)/shard_map/psum | solution.py:128
  320.2 21.6 %copy-start = (f32[4,2,256,256]{3,2,1,0:T(8,128)S(1)}, f32[4,2,256,256]{3,2,1,0:T(8,128)}, u32[]{:S(2)}) copy-start(f32[4,2,256,256]{3,2,1,0:T(8,128)} %param.17) | copy-start | bytes 6291460
  320.2 7.1 %collective-permute-start.4 = (f32[2,64,384]{2,1,0:T(8,128)S(1)}, f32[2,64,384]{2,1,0:T(8,128)S(1)}, u32[]{:S(2)}, u32[]{:S(2)}) collective-permute-start(f32[2,64,384]{2,1,0:T(8,128)S(1)} %slice.183), channel_id=1, source_target_pairs={{0,8},{8,16},{16,24},{1,9},{9,17},{17,25},{2,10},{10,18},{18,26},{... | collective-permute-start | bytes 589832 | tf_op jit(solution)/shard_map/ppermute | solution.py:15
  328.1 9.8 %collective-permute-start.5 = (f32[2,64,384]{2,1,0:T(8,128)}, f32[2,64,384]{2,1,0:T(8,128)}, u32[]{:S(2)}, u32[]{:S(2)}) collective-permute-start(f32[2,64,384]{2,1,0:T(8,128)} %get-tuple-element.194), channel_id=1, source_target_pairs={{8,0},{16,8},{24,16},{9,1},{17,9},{25,17},{10,2},{18,10},{26,18},{... | collective-permute-start | bytes 589832 | tf_op jit(solution)/shard_map/ppermute | solution.py:18
  339.7 6.7 %collective-permute-start.6 = (f32[2,256,64]{2,1,0:T(8,128)}, f32[2,256,64]{2,1,0:T(8,128)}, u32[]{:S(2)}, u32[]{:S(2)}) collective-permute-start(f32[2,256,64]{2,1,0:T(8,128)} %get-tuple-element.193), channel_id=1, source_target_pairs={{0,1},{1,2},{2,3},{3,4},{4,5},{5,6},{6,7},{8,9},{9,10},{10,11},{11... | collective-permute-start | bytes 393224 | tf_op jit(solution)/shard_map/ppermute | solution.py:15
  345.1 5.6 %collective-permute-start.7 = (f32[2,256,64]{2,1,0:T(8,128)}, f32[2,256,64]{2,1,0:T(8,128)S(1)}, u32[]{:S(2)}, u32[]{:S(2)}) collective-permute-start(f32[2,256,64]{2,1,0:T(8,128)} %get-tuple-element.192), channel_id=1, source_target_pairs={{1,0},{2,1},{3,2},{4,3},{5,4},{6,5},{7,6},{9,8},{10,9},{11,10},{12... | collective-permute-start | bytes 393224 | tf_op jit(solution)/shard_map/ppermute | solution.py:18
Sparse Core Ops, SparseCore 0:
  138.5 71.4 all-reduce.4
  212.5 93.9 all-reduce.6
